TPU v7x, 256 devices: a whole 4x4x8 slice. The times are simulated.
256 devices in a mesh: lag: 8 (over y, z_lo), row: 32 (over z_hi, x, core).
Axes of the slice: x: 4, y: 4, z: 8 (z_hi: 4, z_lo: 2; z = z_hi * 2 + z_lo), core: 2. Of those that a mesh axis runs over, the one named last changes fastest.
Arguments:
- lag_matrices: bfloat16 [8, 8192, 8192], P('lag', 'row'), may hold values from -0.0234375 to 0.0234375
- history: bfloat16 [8, 8192, 256], P('lag', 'row'), may hold values from -6 to 6
- excitation: float32 [4, 8192, 256], P(None, 'row'), may hold values from -6 to 6
- admittance: float32 [8192], P('row'), may hold values from 0.3 to 1.5
- saturation: float32 [8192], P('row'), may hold values from 0.2 to 1
Outputs:
- densities: bfloat16 [4, 8192, 256], P(None, 'row')
All inputs are finite; a program needn't handle non-finite values.
Results may differ from a plain program's by a relative error of at most 0.0023.
Values may be sent and summed in bfloat16 or wider, within the bound.
A program may use at most 128 MiB of HBM per device.

v0:
```python
import jax
import jax.numpy as jnp
from jax import lax
from jax.sharding import PartitionSpec as P


def passed_along(value, axis, steps):
    count = lax.axis_size(axis)
    initial, last = (max(0, -steps), min(count, count - steps))
    return lax.ppermute(value, axis, [(source, source + steps) for source in range(initial, last)])


def load_update(drive, admit_col, satur_col):
    return (admit_col * drive / jnp.sqrt(1.0 + (satur_col * drive) ** 2)).astype(jnp.bfloat16)


def body(lag_matrices, history, excitation, admittance, saturation):
    slot_count = lag_matrices.shape[0]
    step_count = excitation.shape[0]
    lag_index = lax.axis_index("lag")
    admit_col = admittance[:, None]
    satur_col = saturation[:, None]
    history_now = history
    results = []
    for step_index in range(step_count):
        partial_sum = jnp.einsum(
            "lrm,lmc->rc",
            lag_matrices,
            lax.all_gather(history_now, "row", axis=1, tiled=True),
            preferred_element_type=jnp.float32,
        )
        summed = lax.psum(partial_sum, "lag")
        density = load_update(excitation[step_index] - summed, admit_col, satur_col)
        results.append(density)
        if step_index + 1 < step_count:
            incoming = passed_along(history_now[slot_count - 1], "lag", 1)
            newest = jnp.where(lag_index == 0, density, incoming)
            history_now = jnp.concatenate([newest[None], history_now[:-1]], axis=0)
    return jnp.stack(results)


def solution(mesh):
    placed = (
        P("lag", "row", None),
        P("lag", "row", None),
        P(None, "row", None),
        P("row"),
        P("row"),
    )
    return jax.shard_map(
        body, mesh=mesh, in_specs=placed, out_specs=P(None, "row", None), check_vma=False
    )
```

profile of v0, /device:TPU:1, one launch (start us, length us, event | category | flops | bytes accessed | tf_op | source)
XLA Modules:
  0.0 593.1 jit_solution(16436640532941216913)
XLA Ops:
  6.5 0.7 all-gather.8.cloned.1.call-update
  7.3 0.0 all-reduce.5.cloned.1.call-start
  7.3 67.1 %all-gather.8.cloned.1.call-done = bf16[1,8192,256]{2,1,0:T(8,128)(2,1)} async-done(((bf16[1,256,256]{2,1,0:T(8,128)(2,1)}), bf16[1,8192,256]{2,1,0:T(8,128)(2,1)}) %all-gather.8.cloned.1.call-update) | async-done | bytes 4194320 | tf_op jit(solution)/shard_map/all_gather | solution.py:29
  74.4 5.4 fusion
  79.8 0.0 all-reduce.5.cloned.1.call-update
  79.8 0.0 all-gather.10.cloned.1.call-start
  79.9 2.3 collective-permute-start
  82.2 2.5 collective-permute-done
  84.8 66.7 %all-reduce.5.cloned.1.call-done = f32[256,256]{1,0:T(8,128)} async-done(((f32[256,256]{1,0:T(8,128)}), f32[256,256]{1,0:T(8,128)}) %all-reduce.5.cloned.1.call-update) | async-done | bytes 262160 | tf_op jit(solution)/shard_map/psum | solution.py:32
  151.5 1.8 broadcast_select_fusion.2
  153.3 0.0 all-reduce.7.cloned.1.call-start
  153.4 65.4 %all-gather.10.cloned.1.call-done = bf16[8192,256]{1,0:T(8,128)(2,1)} async-done(((bf16[256,256]{1,0:T(8,128)(2,1)}), bf16[8192,256]{1,0:T(8,128)(2,1)}) %all-gather.10.cloned.1.call-update) | async-done | bytes 4194320 | tf_op jit(solution)/shard_map/all_gather | solution.py:29
  218.8 5.4 fusion.15
  224.2 0.0 all-gather.12.cloned.1.call-start
  224.3 2.3 collective-permute-start.1
  226.6 2.5 collective-permute-done.1
  229.1 66.7 %all-reduce.7.cloned.1.call-done = f32[256,256]{1,0:T(8,128)} async-done(((f32[256,256]{1,0:T(8,128)}), f32[256,256]{1,0:T(8,128)}) %all-reduce.7.cloned.1.call-update) | async-done | bytes 262160 | tf_op jit(solution)/shard_map/psum | solution.py:32
  295.8 1.8 broadcast_select_fusion.1
  297.6 0.0 all-reduce.9.cloned.1.call-start
  297.7 65.3 %all-gather.12.cloned.1.call-done = bf16[8192,256]{1,0:T(8,128)(2,1)} async-done(((bf16[256,256]{1,0:T(8,128)(2,1)}), bf16[8192,256]{1,0:T(8,128)(2,1)}) %all-gather.12.cloned.1.call-update) | async-done | bytes 4194320 | tf_op jit(solution)/shard_map/all_gather | solution.py:29
  362.9 5.4 fusion.12
  368.4 0.0 all-gather.14.cloned.1.call-start
  368.4 2.3 collective-permute-start.2
  370.7 2.5 collective-permute-done.2
  373.3 66.7 %all-reduce.9.cloned.1.call-done = f32[256,256]{1,0:T(8,128)} async-done(((f32[256,256]{1,0:T(8,128)}), f32[256,256]{1,0:T(8,128)}) %all-reduce.9.cloned.1.call-update) | async-done | bytes 262160 | tf_op jit(solution)/shard_map/psum | solution.py:32
  440.0 1.8 broadcast_select_fusion
  441.8 0.0 all-reduce.11.cloned.1.call-start
  441.8 65.4 %all-gather.14.cloned.1.call-done = bf16[8192,256]{1,0:T(8,128)(2,1)} async-done(((bf16[256,256]{1,0:T(8,128)(2,1)}), bf16[8192,256]{1,0:T(8,128)(2,1)}) %all-gather.14.cloned.1.call-update) | async-done | bytes 4194320 | tf_op jit(solution)/shard_map/all_gather | solution.py:29
  507.3 5.4 fusion.9
  512.7 71.7 %all-reduce.11.cloned.1.call-done = f32[256,256]{1,0:T(8,128)} async-done(((f32[256,256]{1,0:T(8,128)}), f32[256,256]{1,0:T(8,128)}) %all-reduce.11.cloned.1.call-update) | async-done | bytes 262160 | tf_op jit(solution)/shard_map/psum | solution.py:32
  584.4 1.1 fusion.18
  585.4 0.9 pad_maximum_fusion
  (19 shorter events, 0.1 us)
Async XLA Ops:
  6.5 67.9 %all-gather.8.cloned.1.call-start = ((), (), s32[]{:S(2)}) async-start(), calls=%async_computation | async-start | bytes 4325376 | tf_op jit(solution)/shard_map/all_gather | solution.py:29
  7.3 72.6 %copy-start.3 = (bf16[1,256,256]{2,1,0:T(8,128)(2,1)S(1)}, bf16[1,256,256]{2,1,0:T(8,128)(2,1)}, u32[]{:S(2)}) copy-start(bf16[1,256,256]{2,1,0:T(8,128)(2,1)} %param.6) | copy-start | bytes 393220
  7.3 144.2 %copy-start = (f32[4,256,256]{2,1,0:T(8,128)S(1)}, f32[4,256,256]{2,1,0:T(8,128)}, u32[]{:S(2)}) copy-start(f32[4,256,256]{2,1,0:T(8,128)} %param.7) | copy-start | bytes 3145732
  7.3 144.2 %copy-start.4 = (f32[256]{0:T(256)S(1)}, f32[256]{0:T(256)}, u32[]{:S(2)}) copy-start(f32[256]{0:T(256)} %param.9) | copy-start | bytes 3076
  7.3 144.2 %copy-start.5 = (f32[256]{0:T(256)S(1)}, f32[256]{0:T(256)}, u32[]{:S(2)}) copy-start(f32[256]{0:T(256)} %param.8) | copy-start | bytes 3076
  7.3 144.2 %all-reduce.5.cloned.1.call-start = ((), (), s32[]{:S(2)}) async-start(), calls=%async_computation.1 | async-start | bytes 524288 | tf_op jit(solution)/shard_map/psum | solution.py:32
  79.8 138.9 %all-gather.10.cloned.1.call-start = ((), (), s32[]{:S(2)}) async-start(), calls=%async_computation.5 | async-start | bytes 4325376 | tf_op jit(solution)/shard_map/all_gather | solution.py:29
  79.9 4.9 collective-permute-start
  153.3 71.0 %copy-start.1 = (bf16[256,256]{1,0:T(8,128)(2,1)S(1)}, bf16[256,256]{1,0:T(8,128)(2,1)}, u32[]{:S(2)}) copy-start(bf16[256,256]{1,0:T(8,128)(2,1)} %get-tuple-element.9) | copy-start | bytes 393220
  153.3 142.5 %all-reduce.7.cloned.1.call-start = ((), (), s32[]{:S(2)}) async-start(), calls=%async_computation.2 | async-start | bytes 524288 | tf_op jit(solution)/shard_map/psum | solution.py:32
  224.2 138.7 %all-gather.12.cloned.1.call-start = ((), (), s32[]{:S(2)}) async-start(), calls=%async_computation.6 | async-start | bytes 4325376 | tf_op jit(solution)/shard_map/all_gather | solution.py:29
  224.3 4.8 collective-permute-start.1
  297.6 70.8 %copy-start.2 = (bf16[256,256]{1,0:T(8,128)(2,1)S(1)}, bf16[256,256]{1,0:T(8,128)(2,1)}, u32[]{:S(2)}) copy-start(bf16[256,256]{1,0:T(8,128)(2,1)} %get-tuple-element.7) | copy-start | bytes 393220
  297.6 142.4 %all-reduce.9.cloned.1.call-start = ((), (), s32[]{:S(2)}) async-start(), calls=%async_computation.3 | async-start | bytes 524288 | tf_op jit(solution)/shard_map/psum | solution.py:32
  368.4 138.9 %all-gather.14.cloned.1.call-start = ((), (), s32[]{:S(2)}) async-start(), calls=%async_computation.7 | async-start | bytes 4325376 | tf_op jit(solution)/shard_map/all_gather | solution.py:29
  368.4 4.8 collective-permute-start.2
  441.8 142.6 %all-reduce.11.cloned.1.call-start = ((), (), s32[]{:S(2)}) async-start(), calls=%async_computation.4 | async-start | bytes 524288 | tf_op jit(solution)/shard_map/psum | solution.py:32
Sparse Core Ops, SparseCore 0:
  9.9 64.4 all-gather.7
  80.0 71.4 all-reduce.4
  154.1 64.6 all-gather.9
  224.3 71.4 all-reduce.6
  298.2 64.6 all-gather.11
  368.5 71.4 all-reduce.8
  442.6 64.6 all-gather.13
  512.8 71.4 all-reduce.10
where the time goes:
time: 598 us; the launch traced here: 593 us
  waiting for transfers between devices  543 us (91%)
  matrix products  21.7 us (4%)
  between operations  13.6 us (2%)
  other arithmetic  7.21 us (1%)
  starting transfers between devices  7.18 us (1%)
    psum x4, waiting for transfers between devices, body(): summed = lax.psum(partial_sum, 'lag')  272 us
    all_gather x4, waiting for transfers between devices, body(): lax.all_gather(history_now, 'row', axis=1, tiled=True)  263 us
    dot_general x4, matrix products, body(): jnp.einsum('lrm,lmc->rc', lag_matrices, lax.all_gather(history_now, 'row'...  21.7 us
  transfers between devices with their start and end apart: 11, of which 11 were waited for; matrix products, arithmetic and copies ran while one was open for 0% of the time, Pallas kernels for 0%

commit v1 on v0

v1 whole, which is shorter than its diff:
```python
import functools

import jax
import jax.numpy as jnp
from jax import lax
from jax.experimental import pallas as pl
from jax.experimental.pallas import tpu as pltpu
from jax.sharding import PartitionSpec as P

MESH = pl.DeviceIdType.MESH
STEPS = 4
LAGS = 8
BLOCK = 256
COLS = 256
PIECE = 32
CHUNK = 1024
NEW = 3


def kernel(
    z_hbm, h_hbm, e_hbm, adm_ref, sat_ref, out_hbm,
    zv, zp, wv, pm, gath, part, rsb, dv, ob, ev,
    s_loc, s_shift, r_shift, s_a, r_z, r_x, r_c, s_w, r_w, s_rs, r_rs, s_d, r_dz, r_dx, r_dc, s_o, r_o, s_out,
):
    lag = lax.axis_index("lag")
    row = lax.axis_index("row")
    zh, x, c = row // 8, (row // 2) % 4, row % 2

    def at(zh_, x_, c_):
        return (lag, zh_ * 8 + x_ * 2 + c_)

    zn = [(zh + k) % 4 for k in range(4)]
    xn = [(x + k) % 4 for k in range(4)]
    up_z, down_z, far_z = at(zn[1], x, c), at(zn[3], x, c), at(zn[2], x, c)
    up_x, down_x, far_x = at(zh, xn[1], c), at(zh, xn[3], c), at(zh, xn[2], c)
    mate = at(zh, x, 1 - c)

    def lag_of(k):
        return (lag + k) % LAGS

    def chunk_of(x_, c_):
        return pl.multiple_of((c_ * 4 + x_) * CHUNK, CHUNK)

    def block_at(zh_, x_, c_):
        return pl.multiple_of(chunk_of(x_, c_) + zh_ * BLOCK, BLOCK)

    def send(src, dst, ss, rs, dev):
        pltpu.make_async_remote_copy(
            src_ref=src, dst_ref=dst, send_sem=ss, recv_sem=rs, device_id=dev, device_id_type=MESH
        ).start()

    def wait(ref, sem):
        pltpu.make_async_copy(ref, ref, sem).wait()

    own = block_at(zh, x, c)
    load_h = pltpu.make_async_copy(h_hbm.at[0], gath.at[0, pl.ds(own, BLOCK)], s_loc.at[0])
    load_h.start()

    def load_z(i, _):
        place = pl.multiple_of(((i % 2) * 16 + ((i // 2) % 4) * 4 + i // 8) * BLOCK, BLOCK)
        pltpu.make_async_copy(
            z_hbm.at[0, :, pl.ds(pl.multiple_of(i * BLOCK, BLOCK), BLOCK)],
            zv.at[:, pl.ds(place, BLOCK)],
            s_loc.at[1],
        ).start()
        return 0

    lax.fori_loop(0, 32, load_z, 0)
    piece = pl.multiple_of(lag * PIECE, PIECE)
    load_e = pltpu.make_async_copy(e_hbm.at[:, pl.ds(piece, PIECE)], ev, s_loc.at[2])
    load_e.start()

    barrier = pltpu.get_barrier_semaphore()
    partners = [up_z, down_z, far_z, up_x, down_x, far_x, mate] + [(lag_of(k), row) for k in range(1, LAGS)]
    for dev in partners:
        pl.semaphore_signal(barrier, inc=1, device_id=dev, device_id_type=MESH)
    part[...] = jnp.zeros_like(part)
    lanes = lax.broadcasted_iota(jnp.int32, (PIECE, BLOCK), 1)
    rows_ = lax.broadcasted_iota(jnp.int32, (PIECE, BLOCK), 0) + lag * PIECE
    mine = lanes == rows_
    admit = jnp.sum(jnp.where(mine, adm_ref[...], 0.0), axis=1, keepdims=True)
    satur = jnp.sum(jnp.where(mine, sat_ref[...], 0.0), axis=1, keepdims=True)
    pl.semaphore_wait(barrier, len(partners))

    tasks = []

    def task(t, fn, cond=None):
        tasks.append((t, fn, cond))

    def g(s, start, size):
        return gath.at[s, pl.ds(start, size)]

    def x_send(s, b, zz):
        src = g(s, block_at(zz, x, c), BLOCK)
        send(src, src, s_a.at[s], r_x.at[s, 0, b], up_x)
        send(src, src, s_a.at[s], r_x.at[s, 1, b], down_x)

    def a_start(s):
        if s == 0:
            load_h.wait()
        else:
            wait(g(s, own, BLOCK), r_shift.at[s])
        src = g(s, own, BLOCK)
        send(src, src, s_a.at[s], r_z.at[s, 0], up_z)
        send(src, src, s_a.at[s], r_z.at[s, 1], down_z)
        x_send(s, 0, zh)

    def shift():
        for s in range(1, STEPS):
            @pl.when(lag + s < LAGS)
            def _():
                send(g(0, own, BLOCK), g(s, own, BLOCK), s_shift.at[s], r_shift.at[s], (lag_of(s), row))

    HALF = BLOCK // 2

    def a_z_low(s):
        wait(g(s, block_at(zn[3], x, c), BLOCK), r_z.at[s, 0])
        src = g(s, block_at(zn[3], x, c), HALF)
        send(src, src, s_a.at[s], r_z.at[s, 2], up_z)
        x_send(s, 1, zn[3])

    def a_z_high(s):
        wait(g(s, block_at(zn[1], x, c), BLOCK), r_z.at[s, 1])
        src = g(s, block_at(zn[1], x, c) + HALF, HALF)
        send(src, src, s_a.at[s], r_z.at[s, 2], down_z)
        x_send(s, 2, zn[1])

    def to_mate(s, j, x_):
        src = g(s, chunk_of(x_, c), CHUNK)
        send(src, src, s_a.at[s], r_c.at[s, j], mate)

    def a_z_far(s):
        wait(g(s, block_at(zn[2], x, c), BLOCK), r_z.at[s, 2])
        x_send(s, 3, zn[2])
        to_mate(s, 0, x)

    order = [0, 3, 1, 2]

    def a_x(s, b):
        zz = zn[order[b]]
        wait(g(s, block_at(zz, xn[3], c), BLOCK), r_x.at[s, 0, b])
        src = g(s, block_at(zz, xn[3], c), HALF)
        send(src, src, s_a.at[s], r_x.at[s, 2, b], up_x)
        wait(g(s, block_at(zz, xn[1], c), BLOCK), r_x.at[s, 1, b])
        src = g(s, block_at(zz, xn[1], c) + HALF, HALF)
        send(src, src, s_a.at[s], r_x.at[s, 2, b], down_x)
        if b == 3:
            to_mate(s, 1, xn[3])
            to_mate(s, 2, xn[1])

    def a_x_far(s):
        for b in range(4):
            wait(g(s, block_at(zn[order[b]], xn[2], c), BLOCK), r_x.at[s, 2, b])
        to_mate(s, 3, xn[2])

    def multiply(s, js):
        for j in js:
            wait(g(s, chunk_of(xn[order[j]], 1 - c), CHUNK), r_c.at[s, j])

        def body(t, _):
            step = 2 if js == [3] else 3 * (t // 2) + 3 * (t // 4)
            at_ = chunk_of((x + step) % 4, t % 2)
            part[s] += jnp.dot(
                zv[:, pl.ds(at_, CHUNK)], gath[s, pl.ds(at_, CHUNK), :], preferred_element_type=jnp.float32
            )
            return 0

        lax.fori_loop(0, 2 * len(js), body, 0)

    def a_first(s):
        multiply(s, [0, 1, 2])

    def a_last(s):
        multiply(s, [3])

    def w_send():
        a = lax.broadcasted_iota(jnp.int32, (CHUNK, CHUNK), 0)
        b = lax.broadcasted_iota(jnp.int32, (CHUNK, CHUNK), 1)
        from_ = ((b // PIECE) % 4) * BLOCK + (b // 128) * PIECE + b % PIECE
        pm[...] = jnp.where(a == from_, 1.0, 0.0).astype(jnp.bfloat16)

        def body(q, _):
            picked = jnp.dot(
                zv[:, pl.ds(pl.multiple_of(q * CHUNK, CHUNK), CHUNK)], pm[...], preferred_element_type=jnp.float32
            ).astype(jnp.bfloat16)
            for k in range(LAGS):
                zp[k, :, pl.ds(pl.multiple_of(q * 128, 128), 128)] = picked[:, k * 128 : (k + 1) * 128]
            return 0

        lax.fori_loop(0, LAGS, body, 0)
        pltpu.make_async_copy(zp.at[lag], wv.at[lag], r_w.at[lag]).start()
        for k in range(1, LAGS):
            send(zp.at[lag_of(k)], wv.at[lag], s_w.at[0], r_w.at[lag], (lag_of(k), row))

    def rs_send(n):
        for k in range(1, LAGS):
            to = lag_of(k)
            send(
                part.at[n, pl.ds(pl.multiple_of(to * PIECE, PIECE), PIECE)],
                rsb.at[n, lag], s_rs.at[n], r_rs.at[n], (to, row),
            )
        rsb[n, lag] = part[n, pl.ds(piece, PIECE), :]

    def d_at(zh_, x_):
        return pl.multiple_of((c * 4 + x_) * 128 + zh_ * PIECE, PIECE)

    def new_density(n):
        wait(rsb.at[n, pl.ds(0, LAGS - 1)], r_rs.at[n])
        total = rsb[n, 0]
        for k in range(1, LAGS):
            total = total + rsb[n, k]
        drive = ev[n] - total
        density = (admit * drive / jnp.sqrt(1.0 + (satur * drive) ** 2)).astype(jnp.bfloat16)
        ob[n, pl.ds(piece, PIECE), :] = density
        if n < STEPS - 1:
            dv[n, pl.ds(d_at(zh, x), PIECE), :] = density
            src = dv.at[n, pl.ds(d_at(zh, x), PIECE)]
            send(src, src, s_d.at[n], r_dz.at[n], far_z)
            send(src, src, s_d.at[n], r_dz.at[n], up_z)
            send(src, src, s_d.at[n], r_dz.at[n], down_z)
        src = ob.at[n, pl.ds(piece, PIECE)]
        for k in range(1, LAGS):
            send(src, src, s_o.at[n], r_o.at[n], (lag_of(k), row))

    def d_chunk(n, x_, c_):
        return dv.at[n, pl.ds(pl.multiple_of((c_ * 4 + x_) * 128, 128), 128)]

    def d_x(n):
        wait(dv.at[n, pl.ds(0, 3 * PIECE)], r_dz.at[n])
        src = d_chunk(n, x, c)
        send(src, src, s_d.at[n], r_dx.at[n], far_x)
        send(src, src, s_d.at[n], r_dx.at[n], up_x)
        send(src, src, s_d.at[n], r_dx.at[n], down_x)

    def d_c(n):
        wait(dv.at[n, pl.ds(0, 3 * 128)], r_dx.at[n])
        src = dv.at[n, pl.ds(pl.multiple_of(c * 512, 512), 512)]
        send(src, src, s_d.at[n], r_dc.at[n], mate)

    def w_mul(n, k):
        part[n + 1 + k] += jnp.dot(wv[k], dv[n], preferred_element_type=jnp.float32)

    def d_first(n):
        wait(dv.at[n, pl.ds(0, 512)], r_dc.at[n])
        if n == 0:
            wait(wv.at[0], r_w.at[0])
        w_mul(n, 0)

    def d_rest(n):
        if n == 0:
            wait(wv.at[1], r_w.at[1])
            wait(wv.at[2], r_w.at[2])
        for k in range(1, STEPS - 1 - n):
            w_mul(n, k)

    task(0, functools.partial(a_start, 0))
    task(0.5, shift)

    def z_ready():
        wait(zv, s_loc.at[1])
        load_e.wait()

    task(1, z_ready)
    task(2, w_send, lag < NEW)
    begin = [0, 8, 22, 36]
    for s in range(STEPS):
        cond = None if s == 0 else (lag >= s)
        t = begin[s]
        if s:
            task(t, functools.partial(a_start, s), cond)
        task(t + 5, functools.partial(a_z_low, s), cond)
        task(t + 5.1, functools.partial(a_z_high, s), cond)
        task(t + 8, functools.partial(a_z_far, s), cond)
        for b in range(4):
            task(t + [6, 10, 12, 16][b], functools.partial(a_x, s, b), cond)
        task(t + 17, functools.partial(a_first, s), cond)
        task(t + 19, functools.partial(a_x_far, s), cond)
        task(t + 20, functools.partial(a_last, s), cond)
    ready = 20.5
    for n in range(STEPS):
        task(ready, functools.partial(rs_send, n))
        task(ready + 4, functools.partial(new_density, n))
        if n < STEPS - 1:
            task(ready + 8, functools.partial(d_x, n))
            task(ready + 11, functools.partial(d_c, n))
            task(ready + 12.5, functools.partial(d_first, n))
            task(ready + 13.5, functools.partial(d_rest, n))
            ready = max(ready + 13, begin[n + 1] + 20.4)
    for t, fn, cond in sorted(tasks, key=lambda item: item[0]):
        if cond is None:
            fn()
        else:
            pl.when(cond)(fn)

    for n in range(STEPS):
        wait(ob.at[n, pl.ds(0, (LAGS - 1) * PIECE)], r_o.at[n])
    store = pltpu.make_async_copy(ob, out_hbm, s_out.at[0])
    store.start()
    for n in range(STEPS):
        wait(rsb.at[n, pl.ds(0, LAGS - 1)], s_rs.at[n])
        wait(ob.at[n, pl.ds(0, (LAGS - 1) * PIECE)], s_o.at[n])
        if n < STEPS - 1:
            wait(dv.at[n, pl.ds(0, 3 * PIECE + 3 * 128 + 512)], s_d.at[n])
    for s in range(STEPS):
        def done(s=s):
            wait(g(s, 0, 3 * BLOCK + 12 * BLOCK + 4 * CHUNK), s_a.at[s])

        if s == 0:
            done()
        else:
            pl.when(lag >= s)(done)

            @pl.when(lag + s < LAGS)
            def _():
                wait(g(0, 0, BLOCK), s_shift.at[s])

    @pl.when(lag < NEW)
    def _():
        wait(zp.at[pl.ds(0, LAGS - 1)], s_w.at[0])

    store.wait()


def body(lag_matrices, history, excitation, admittance, saturation):
    dma = pltpu.SemaphoreType.DMA
    any_ = pl.BlockSpec(memory_space=pl.ANY)
    vmem = pl.BlockSpec(memory_space=pltpu.VMEM)
    return pl.pallas_call(
        kernel,
        out_shape=jax.ShapeDtypeStruct((STEPS, BLOCK, COLS), jnp.bfloat16),
        in_specs=[any_, any_, any_, vmem, vmem],
        out_specs=any_,
        scratch_shapes=[
            pltpu.VMEM((BLOCK, 8192), jnp.bfloat16),
            pltpu.VMEM((LAGS, BLOCK, CHUNK), jnp.bfloat16),
            pltpu.VMEM((NEW, BLOCK, CHUNK), jnp.bfloat16),
            pltpu.VMEM((CHUNK, CHUNK), jnp.bfloat16),
            pltpu.VMEM((STEPS, 8192, COLS), jnp.bfloat16),
            pltpu.VMEM((STEPS, BLOCK, COLS), jnp.float32),
            pltpu.VMEM((STEPS, LAGS, PIECE, COLS), jnp.float32),
            pltpu.VMEM((STEPS - 1, CHUNK, COLS), jnp.bfloat16),
            pltpu.VMEM((STEPS, BLOCK, COLS), jnp.bfloat16),
            pltpu.VMEM((STEPS, PIECE, COLS), jnp.float32),
            dma((3,)),
            dma((STEPS,)), dma((STEPS,)),
            dma((STEPS,)), dma((STEPS, 3)), dma((STEPS, 3, 4)), dma((STEPS, 4)),
            dma((1,)), dma((NEW,)),
            dma((STEPS,)), dma((STEPS,)),
            dma((STEPS,)), dma((STEPS,)), dma((STEPS,)), dma((STEPS,)),
            dma((STEPS,)), dma((STEPS,)),
            dma((1,)),
        ],
        compiler_params=pltpu.CompilerParams(
            collective_id=0, has_side_effects=True, vmem_limit_bytes=60 * 1024 * 1024
        ),
    )(
        lag_matrices, history, excitation, admittance.reshape(1, BLOCK), saturation.reshape(1, BLOCK)
    )


def solution(mesh):
    placed = (
        P("lag", "row", None),
        P("lag", "row", None),
        P(None, "row", None),
        P("row"),
        P("row"),
    )
    return jax.shard_map(
        body, mesh=mesh, in_specs=placed, out_specs=P(None, "row", None), check_vma=False
    )
```

time: 598 us -> 182 us (0.30)
  waiting for transfers between devices: 543 us -> 0 us
  Pallas kernels: 0 us -> 180 us
  matrix products: 21.7 us -> 0 us
  between operations: 13.6 us -> 0.01 us
  other arithmetic: 7.21 us -> 0 us
  starting transfers between devices: 7.18 us -> 0 us
    psum x4 -> x0, waiting for transfers between devices: 272 us -> none  [body(): summed = lax.psum(partial_sum, 'lag')]
    all_gather x4 -> x0, waiting for transfers between devices: 263 us -> none  [body(): lax.all_gather(history_now, 'row', axis=1, tiled=True)]
    pallas_call x0 -> x1, Pallas kernels: none -> 180 us  [body(): pl.pallas_call(kernel, out_shape=jax.ShapeDtypeStruct((STEPS, BLOCK, COLS...]
    dot_general x4 -> x0, matrix products: 21.7 us -> none  [body(): jnp.einsum('lrm,lmc->rc', lag_matrices, lax.all_gather(history_now, 'row'...]
    ppermute x3 -> x0, waiting for transfers between devices: 7.64 us -> none  [passed_along(): lax.ppermute(value, axis, [(source, source + steps) for source in range(i...]
    ppermute x3 -> x0, starting transfers between devices: 6.89 us -> none  [passed_along(): lax.ppermute(value, axis, [(source, source + steps) for source in range(i...]
  transfers between devices with their start and end apart: 11 -> 0, of which waited for: 11 -> 0; matrix products, arithmetic and copies ran while one was open for 0% -> 0% of each run, Pallas kernels for 0% -> 0%
where the time goes in v1:
time: 182 us
  Pallas kernels  180 us (99%)
  local copies, waits for them, and re-layouts  1.87 us (1%)
    pallas_call x1, Pallas kernels, body(): pl.pallas_call(kernel, out_shape=jax.ShapeDtypeStruct((STEPS, BLOCK, COLS...  180 us

profile of v1, /device:TPU:1, one launch (start us, length us, event | category | flops | bytes accessed | tf_op | source)
XLA Modules:
  0.0 181.7 jit_solution(16018997033026871166)
XLA Ops:
  0.0 179.8 %shard_map.55 = bf16[4,256,256]{2,1,0:T(8,128)(2,1)} custom-call(bf16[1,256,8192]{2,1,0:T(8,128)(2,1)} %z_hbm.1, bf16[1,256,256]{2,1,0:T(8,128)(2,1)} %h_hbm.1, f32[4,256,256]{2,1,0:T(8,128)} %e_hbm.1, f32[1,256]{1,0:T(1,128)} %bitcast.2, f32[1,256]{1,0:T(1,128)} %bitcast.3), custom_call_target="tpu_custom_call" | custom-call | tf_op jit(solution)/shard_map/pallas_call | solution.py:328
  179.8 1.9 %copy.7 = bf16[4,256,256]{2,1,0:T(8,128)(2,1)} copy(bf16[4,256,256]{2,1,0:T(8,128)(2,1)} %shard_map.55) | data formatting | bytes 1048576

commit v2 on v1

v2 whole, which is shorter than its diff:
```python
import functools

import jax
import jax.numpy as jnp
from jax import lax
from jax.experimental import pallas as pl
from jax.experimental.pallas import tpu as pltpu
from jax.sharding import PartitionSpec as P

MESH = pl.DeviceIdType.MESH
STEPS = 4
LAGS = 8
BLOCK = 256
COLS = 256
ZT = (0, 7, 7.1, 11)
Z_AT = (0, 13, 39.2, 57.2)
X_AT = ((0, 8, 12, 17), (23, 27, 31, 35), (46, 50, 54, 58), (62, 66, 70, 74))
X_LAG = 5
Y_AT = (26, 3, 6)
C_AT = (26, 45, 62, 79)
W_RELAY = 20
PIECE = 32
CHUNK = 1024


def kernel(
    z_hbm, h_hbm, e_hbm, adm_ref, sat_ref, out_hbm,
    zv, zp, wv, gath, part, rsb, dv, ob, ev,
    s_loc, s_shift, r_shift, s_a, r_z, r_x, r_c, s_y, r_y, s_w, r_w, s_rs, r_rs, s_d, r_dz, r_dx, r_dc, s_o, r_o, s_out,
):
    lag = lax.axis_index("lag")
    row = lax.axis_index("row")
    zh, x, c = row // 8, (row // 2) % 4, row % 2

    def at(zh_, x_, c_):
        return (lag, zh_ * 8 + x_ * 2 + c_)

    zn = [(zh + k) % 4 for k in range(4)]
    xn = [(x + k) % 4 for k in range(4)]
    up_z, down_z, far_z = at(zn[1], x, c), at(zn[3], x, c), at(zn[2], x, c)
    up_x, down_x, far_x = at(zh, xn[1], c), at(zh, xn[3], c), at(zh, xn[2], c)
    mate = at(zh, x, 1 - c)

    def lag_of(k):
        return (lag + k) % LAGS

    def chunk_of(x_, c_):
        return pl.multiple_of((c_ * 4 + x_) * CHUNK, CHUNK)

    def block_at(zh_, x_, c_):
        return pl.multiple_of(chunk_of(x_, c_) + zh_ * BLOCK, BLOCK)

    def send(src, dst, ss, rs, dev):
        pltpu.make_async_remote_copy(
            src_ref=src, dst_ref=dst, send_sem=ss, recv_sem=rs, device_id=dev, device_id_type=MESH
        ).start()

    def wait(ref, sem):
        pltpu.make_async_copy(ref, ref, sem).wait()

    own = block_at(zh, x, c)
    load_h = pltpu.make_async_copy(h_hbm.at[0], gath.at[0, pl.ds(own, BLOCK)], s_loc.at[0])
    load_h.start()

    def load_z(i, _):
        place = pl.multiple_of(((i % 2) * 16 + ((i // 2) % 4) * 4 + i // 8) * BLOCK, BLOCK)
        pltpu.make_async_copy(
            z_hbm.at[0, :, pl.ds(pl.multiple_of(i * BLOCK, BLOCK), BLOCK)],
            zv.at[:, pl.ds(place, BLOCK)],
            s_loc.at[1],
        ).start()
        return 0

    lax.fori_loop(0, 32, load_z, 0)
    piece = pl.multiple_of(lag * PIECE, PIECE)
    load_e = pltpu.make_async_copy(e_hbm.at[:, pl.ds(piece, PIECE)], ev, s_loc.at[2])
    load_e.start()

    barrier = pltpu.get_barrier_semaphore()
    partners = [up_z, down_z, far_z, up_x, down_x, far_x, mate] + [(lag_of(k), row) for k in range(1, LAGS)]
    for dev in partners:
        pl.semaphore_signal(barrier, inc=1, device_id=dev, device_id_type=MESH)
    part[...] = jnp.zeros_like(part)
    lanes = lax.broadcasted_iota(jnp.int32, (PIECE, BLOCK), 1)
    rows_ = lax.broadcasted_iota(jnp.int32, (PIECE, BLOCK), 0) + lag * PIECE
    mine = lanes == rows_
    admit = jnp.sum(jnp.where(mine, adm_ref[...], 0.0), axis=1, keepdims=True)
    satur = jnp.sum(jnp.where(mine, sat_ref[...], 0.0), axis=1, keepdims=True)
    pl.semaphore_wait(barrier, len(partners))

    order = [0, 3, 1, 2]
    tasks = []

    def task(t, fn, cond=None):
        tasks.append((t, fn, cond))

    def g(s, start, size):
        return gath.at[s, pl.ds(start, size)]

    def x_send(s, b):
        src = g(s, block_at(zn[order[b]], x, c), BLOCK)
        send(src, src, s_a.at[s], r_x.at[s, 0, b], up_x)
        send(src, src, s_a.at[s], r_x.at[s, 1, b], down_x)

    def a_start(s):
        if s == 0:
            load_h.wait()
        elif s < 3:
            @pl.when(lag >= s)
            def _():
                wait(g(s, own, BLOCK), r_shift.at[s])
        if s >= 2:
            @pl.when(lag == s - 1)
            def _():
                gath[s, pl.ds(own, BLOCK), :] = ob[0]
        if s == 3:
            @pl.when(lag == 1)
            def _():
                gath[s, pl.ds(own, BLOCK), :] = ob[1]

        src = g(s, own, BLOCK)
        send(src, src, s_a.at[s], r_z.at[s, 0], up_z)
        send(src, src, s_a.at[s], r_z.at[s, 1], down_z)
        send(src, src, s_a.at[s], r_z.at[s, 2], far_z)

    def shift():
        for s in (1, 2):
            @pl.when(lag + s < LAGS)
            def _():
                send(g(0, own, BLOCK), g(s, own, BLOCK), s_shift.at[s], r_shift.at[s], (lag_of(s), row))

    HALF = BLOCK // 2

    def to_mate(s, j, x_):
        src = g(s, chunk_of(x_, c), CHUNK)
        send(src, src, s_a.at[s], r_c.at[s, j], mate)

    def to_y(j, b):
        start = block_at(zn[order[b]], xn[order[j]], c)
        send(g(1, start, BLOCK), g(3, start, BLOCK), s_y.at[0], r_y.at[(0, 1, 1, 2)[j]], (lag_of(2), row))

    def from_y(i):
        wait(g(3, 0, (1, 2, 1)[i] * CHUNK), r_y.at[i])
        for j in ((0,), (1, 2), (3,))[i]:
            to_mate(3, j, xn[order[j]])

    def a_z(s, b):
        wait(g(s, block_at(zn[order[b]], x, c), BLOCK), r_z.at[s, b - 1])
        if b == 3:
            to_mate(s, 0, x)

    def a_x(s, b):
        zz = zn[order[b]]
        wait(g(s, block_at(zz, xn[3], c), BLOCK), r_x.at[s, 0, b])
        src = g(s, block_at(zz, xn[3], c), HALF)
        send(src, src, s_a.at[s], r_x.at[s, 2, b], up_x)
        wait(g(s, block_at(zz, xn[1], c), BLOCK), r_x.at[s, 1, b])
        src = g(s, block_at(zz, xn[1], c) + HALF, HALF)
        send(src, src, s_a.at[s], r_x.at[s, 2, b], down_x)
        if b == 3:
            to_mate(s, 1, xn[3])
            to_mate(s, 2, xn[1])

    def a_x_far(s):
        for b in range(4):
            wait(g(s, block_at(zn[order[b]], xn[2], c), BLOCK), r_x.at[s, 2, b])
        to_mate(s, 3, xn[2])

    def multiply(s, j):
        wait(g(s, chunk_of(xn[order[j]], 1 - c), CHUNK), r_c.at[s, j])

        def body(t, _):
            at_ = chunk_of(xn[order[j]], t)
            part[s] += jnp.dot(
                zv[:, pl.ds(at_, CHUNK)], gath[s, pl.ds(at_, CHUNK), :], preferred_element_type=jnp.float32
            )
            return 0

        lax.fori_loop(0, 2, body, 0)

    def w_cut():
        place = lax.broadcasted_iota(jnp.int32, (BLOCK, 128), 1) // PIECE

        def body(q, _):
            for half in range(2):
                tiles = []
                for b in range(4):
                    at_ = pl.multiple_of(q * CHUNK + b * BLOCK + half * 128, 128)
                    tile = zv[:, pl.ds(at_, 128)].astype(jnp.float32)
                    tiles.append(pltpu.roll(tile, PIECE * b, 1) if b else tile)
                for a in range(4):
                    got = tiles[(0 - a) % 4]
                    for p in range(1, 4):
                        got = jnp.where(place == p, tiles[(p - a) % 4], got)
                    zp[4 * half + a, :, pl.ds(pl.multiple_of(q * 128, 128), 128)] = got.astype(jnp.bfloat16)
            return 0

        lax.fori_loop(0, LAGS, body, 0)

    def w_send():
        pltpu.make_async_copy(zp.at[0], wv, r_w.at[0]).start()
        for k in (3, 7):
            send(zp.at[k], zp.at[0], s_w.at[0], r_w.at[1], (k - 1, row))
        for k in (4, 5, 2, 6, 1):
            send(zp.at[k], wv, s_w.at[0], r_w.at[0], (k, row))

    def w_relay():
        wait(zp.at[0], r_w.at[1])
        send(zp.at[0], wv, s_w.at[0], r_w.at[0], (lag_of(1), row))

    def rs_send(n):
        for k in range(1, LAGS):
            to = lag_of(k)
            send(
                part.at[n, pl.ds(pl.multiple_of(to * PIECE, PIECE), PIECE)],
                rsb.at[n, lag], s_rs.at[n], r_rs.at[n], (to, row),
            )
        rsb[n, lag] = part[n, pl.ds(piece, PIECE), :]

    def d_at(zh_, x_):
        return pl.multiple_of((c * 4 + x_) * 128 + ((zh_ + lag) % 4) * PIECE, PIECE)

    def new_density(n):
        wait(rsb.at[n, pl.ds(0, LAGS - 1)], r_rs.at[n])
        total = rsb[n, 0]
        for k in range(1, LAGS):
            total = total + rsb[n, k]
        drive = ev[n] - total
        density = (admit * drive / jnp.sqrt(1.0 + (satur * drive) ** 2)).astype(jnp.bfloat16)
        ob[n, pl.ds(piece, PIECE), :] = density
        if n < STEPS - 1:
            dv[n, pl.ds(d_at(zh, x), PIECE), :] = density
            src = dv.at[n, pl.ds(d_at(zh, x), PIECE)]
            send(src, src, s_d.at[n], r_dz.at[n, 0], far_z)
            send(src, src, s_d.at[n], r_dz.at[n, 1], up_z)
            send(src, src, s_d.at[n], r_dz.at[n, 2], down_z)
            d_send_x(n, 0)
        src = ob.at[n, pl.ds(piece, PIECE)]
        for k in range(1, LAGS):
            send(src, src, s_o.at[n], r_o.at[n], (lag_of(k), row))

    def d_send_x(n, b):
        src = d_piece(n, b)
        for dev in (far_x, up_x, down_x):
            send(src, src, s_d.at[n], r_dx.at[n, b], dev)

    def d_piece(n, b):
        return dv.at[n, pl.ds(d_at(zn[order[b]], x), PIECE)]

    def d_near(n):
        wait(d_piece(n, 1), r_dz.at[n, 1])
        d_send_x(n, 1)
        wait(d_piece(n, 2), r_dz.at[n, 2])
        d_send_x(n, 2)

    def d_far(n):
        wait(d_piece(n, 3), r_dz.at[n, 0])
        d_send_x(n, 3)

    def d_c(n):
        for b in range(4):
            wait(dv.at[n, pl.ds(0, 3 * PIECE)], r_dx.at[n, b])
        src = dv.at[n, pl.ds(pl.multiple_of(c * 512, 512), 512)]
        send(src, src, s_d.at[n], r_dc.at[n], mate)

    def d_mul(n):
        wait(dv.at[n, pl.ds(0, 512)], r_dc.at[n])
        if n == 0:
            wait(wv, r_w.at[0])
        part[n + 1] += jnp.dot(wv[...], dv[n], preferred_element_type=jnp.float32)

    def o_ready(n):
        wait(ob.at[n, pl.ds(0, (LAGS - 1) * PIECE)], r_o.at[n])

    def z_ready():
        wait(zv, s_loc.at[1])
        load_e.wait()

    ends = [0] * STEPS

    def gather(s, tz, x_at, x_lag, cond=None):
        def add(t, fn, *more):
            task(t, functools.partial(fn, s, *more), cond)

        add(tz, a_start)
        for b in range(1, 4):
            add(tz + ZT[b], a_z, b)
        add(tz + ZT[3] + 2, multiply, 0)
        for b in range(4):
            add(max(x_at[b], tz + ZT[b]) + 0.001, x_send, b)
            add(x_at[b] + x_lag, a_x, b)
        last = x_at[3] + x_lag
        add(last + 1.5, multiply, 1)
        add(last + 1.6, multiply, 2)
        add(last + 2, a_x_far)
        add(last + 3.5, multiply, 3)
        ends[s] = max(ends[s], last + 3.6)

    gather(0, 0, X_AT[0], 5)
    task(0.5, shift)
    task(1, z_ready)
    task(1.1, w_cut, lag == 0)
    task(1.2, w_send, lag == 0)
    task(W_RELAY, w_relay, (lag == 2) | (lag == 6))
    gather(1, Z_AT[1], X_AT[1], X_LAG, lag >= 1)
    gather(2, Z_AT[2], X_AT[2], X_LAG, lag >= 1)
    gather(3, Z_AT[3], X_AT[3], X_LAG, (lag == 1) | (lag == 2))
    blocks = [(0, b) for b in range(4)] + [(j, b) for b in range(4) for j in (1, 2)] + [(3, b) for b in range(4)]
    for i, (j, b) in enumerate(blocks):
        task(Y_AT[0] + Y_AT[1] * i, functools.partial(to_y, j, b), (lag >= 1) & (lag + 2 < LAGS))
    for i in range(3):
        t = Y_AT[0] + Y_AT[1] * (3, 11, 15)[i] + Y_AT[2]
        task(t, functools.partial(from_y, i), lag >= 3)
        for j in ((0,), (1, 2), (3,))[i]:
            task(t + 2, functools.partial(multiply, 3, j), lag >= 3)
        ends[3] = max(ends[3], t + 2.1)
    for n in range(STEPS):
        ready = max(C_AT[n], ends[n])
        task(ready, functools.partial(rs_send, n))
        task(ready + 6, functools.partial(new_density, n))
        task(ready + 11, functools.partial(o_ready, n))
        if n < STEPS - 1:
            task(ready + 9, functools.partial(d_near, n))
            task(ready + 10.5, functools.partial(d_far, n))
            task(ready + 14, functools.partial(d_c, n))
            task(ready + 15.5, functools.partial(d_mul, n))
            ends[n + 1] = max(ends[n + 1], ready + 15.6)
            if n < 2:
                assert Z_AT[n + 2] > ready + 11
    for t, fn, cond in sorted(tasks, key=lambda item: item[0]):
        if cond is None:
            fn()
        else:
            pl.when(cond)(fn)

    store = pltpu.make_async_copy(ob, out_hbm, s_out.at[0])
    store.start()
    for n in range(STEPS):
        wait(rsb.at[n, pl.ds(0, LAGS - 1)], s_rs.at[n])
        wait(ob.at[n, pl.ds(0, (LAGS - 1) * PIECE)], s_o.at[n])
        if n < STEPS - 1:
            wait(dv.at[n, pl.ds(0, 3 * PIECE + 12 * PIECE + 512)], s_d.at[n])
    for s in range(STEPS):
        def done(s=s):
            wait(g(s, 0, 3 * BLOCK + 12 * BLOCK + 4 * CHUNK), s_a.at[s])

        if s == 0:
            done()
        else:
            pl.when((lag >= 1) & (lag < 3) if s == 3 else lag >= 1)(done)
            if s == 3:
                @pl.when(lag >= 3)
                def _():
                    wait(g(s, 0, 4 * CHUNK), s_a.at[s])
                continue

            @pl.when(lag + s < LAGS)
            def _():
                wait(g(0, 0, BLOCK), s_shift.at[s])

    @pl.when((lag >= 1) & (lag + 2 < LAGS))
    def _():
        wait(g(3, 0, 4 * CHUNK), s_y.at[0])

    @pl.when((lag == 2) | (lag == 6))
    def _():
        wait(zp.at[0], s_w.at[0])

    @pl.when(lag == 0)
    def _():
        wait(zp.at[pl.ds(0, LAGS - 1)], s_w.at[0])

    store.wait()


def body(lag_matrices, history, excitation, admittance, saturation):
    dma = pltpu.SemaphoreType.DMA
    any_ = pl.BlockSpec(memory_space=pl.ANY)
    vmem = pl.BlockSpec(memory_space=pltpu.VMEM)
    return pl.pallas_call(
        kernel,
        out_shape=jax.ShapeDtypeStruct((STEPS, BLOCK, COLS), jnp.bfloat16),
        in_specs=[any_, any_, any_, vmem, vmem],
        out_specs=any_,
        scratch_shapes=[
            pltpu.VMEM((BLOCK, 8192), jnp.bfloat16),
            pltpu.VMEM((LAGS, BLOCK, CHUNK), jnp.bfloat16),
            pltpu.VMEM((BLOCK, CHUNK), jnp.bfloat16),
            pltpu.VMEM((STEPS, 8192, COLS), jnp.bfloat16),
            pltpu.VMEM((STEPS, BLOCK, COLS), jnp.float32),
            pltpu.VMEM((STEPS, LAGS, PIECE, COLS), jnp.float32),
            pltpu.VMEM((STEPS - 1, CHUNK, COLS), jnp.bfloat16),
            pltpu.VMEM((STEPS, BLOCK, COLS), jnp.bfloat16),
            pltpu.VMEM((STEPS, PIECE, COLS), jnp.float32),
            dma((3,)),
            dma((STEPS,)), dma((STEPS,)),
            dma((STEPS,)), dma((STEPS, 3)), dma((STEPS, 3, 4)), dma((STEPS, 4)),
            dma((1,)), dma((3,)),
            dma((1,)), dma((2,)),
            dma((STEPS,)), dma((STEPS,)),
            dma((STEPS,)), dma((STEPS, 3)), dma((STEPS, 4)), dma((STEPS,)),
            dma((STEPS,)), dma((STEPS,)),
            dma((1,)),
        ],
        compiler_params=pltpu.CompilerParams(
            collective_id=0, has_side_effects=True, vmem_limit_bytes=60 * 1024 * 1024
        ),
    )(
        lag_matrices, history, excitation, admittance.reshape(1, BLOCK), saturation.reshape(1, BLOCK)
    )


def solution(mesh):
    placed = (
        P("lag", "row", None),
        P("lag", "row", None),
        P(None, "row", None),
        P("row"),
        P("row"),
    )
    return jax.shard_map(
        body, mesh=mesh, in_specs=placed, out_specs=P(None, "row", None), check_vma=False
    )
```

time: 182 us -> 135 us (0.74)
  Pallas kernels: 180 us -> 133 us
    pallas_call x1, Pallas kernels: 180 us -> 133 us  [body(): pl.pallas_call(kernel, out_shape=jax.ShapeDtypeStruct((STEPS, BLOCK, COLS...]
where the time goes in v2:
time: 135 us
  Pallas kernels  133 us (99%)
  local copies, waits for them, and re-layouts  1.87 us (1%)
    pallas_call x1, Pallas kernels, body(): pl.pallas_call(kernel, out_shape=jax.ShapeDtypeStruct((STEPS, BLOCK, COLS...  133 us

profile of v2, /device:TPU:1, one launch (start us, length us, event | category | flops | bytes accessed | tf_op | source)
XLA Modules:
  0.0 135.2 jit_solution(9939008450789483119)
XLA Ops:
  0.0 133.3 %shard_map.55 = bf16[4,256,256]{2,1,0:T(8,128)(2,1)} custom-call(bf16[1,256,8192]{2,1,0:T(8,128)(2,1)} %z_hbm.1, bf16[1,256,256]{2,1,0:T(8,128)(2,1)} %h_hbm.1, f32[4,256,256]{2,1,0:T(8,128)} %e_hbm.1, f32[1,256]{1,0:T(1,128)} %bitcast.2, f32[1,256]{1,0:T(1,128)} %bitcast.3), custom_call_target="tpu_custom_call" | custom-call | tf_op jit(solution)/shard_map/pallas_call | solution.py:380
  133.4 1.9 %copy.7 = bf16[4,256,256]{2,1,0:T(8,128)(2,1)} copy(bf16[4,256,256]{2,1,0:T(8,128)(2,1)} %shard_map.55) | data formatting | bytes 1048576

commit v3 on v2

--- a/solution.py
+++ b/solution.py
@@ -12,13 +12,30 @@
 LAGS = 8
 BLOCK = 256
 COLS = 256
-ZT = (0, 7, 7.1, 11)
-Z_AT = (0, 13, 39.2, 57.2)
-X_AT = ((0, 8, 12, 17), (23, 27, 31, 35), (46, 50, 54, 58), (62, 66, 70, 74))
-X_LAG = 5
-Y_AT = (26, 3, 6)
-C_AT = (26, 45, 62, 79)
-W_RELAY = 20
+ROUTED = (0,)
+FAR_FIRST = (4, 5, 3, 2, 6, 1, 7)
+ORDER = (
+    ("own", 0), ("start", 0), ("x", 0, 0), "shift", "z", "cut", "cut_out", ("along_z", 0, 1), ("along_z", 0, 2),
+    ("x", 0, 1), ("own", 1), ("start", 1), ("along_z", 0, 3), ("x", 0, 2), ("mul", 0, 0), ("x", 0, 3),
+    ("along_z", 1, 1), ("along_z", 1, 2), ("x", 1, 0), ("y", 0, 0), "relay", ("along_z", 1, 3), ("y", 0, 1),
+    ("x", 1, 1), ("along_x", 0, 0), ("along_x", 0, 1), ("along_x", 0, 2), ("along_x", 0, 3), ("mul", 0, 1),
+    ("mul", 0, 2), ("far_x", 0), ("mul", 0, 3), ("sum", 0), ("y", 0, 2), ("mul", 1, 0), ("x", 1, 2), ("along_x", 1, 0),
+    ("y", 0, 3), ("x", 1, 3), ("along_x", 1, 1), ("density", 0), ("out", 0), ("y", 1, 0), ("near", 0),
+    ("along_x", 1, 2), ("y", 2, 0), ("far", 0), ("outs", 0), ("own", 2), ("start", 2), ("own", 3), ("start", 3),
+    ("y", 1, 1), ("along_x", 1, 3), ("mate", 0), ("along_y", 0), ("mul", 1, 1), ("new", 0), ("mul", 1, 2), ("far_x", 1),
+    ("mul", "y", 0), ("y", 2, 1), ("mul", 1, 3), ("sum", 1), ("x", 2, 0), ("x", 3, 0), ("along_z", 2, 1),
+    ("along_z", 3, 1), ("along_z", 2, 2), ("along_z", 3, 2), ("y", 1, 2), ("x", 2, 1), ("x", 3, 1), ("y", 2, 2),
+    ("along_z", 2, 3), ("along_z", 3, 3), ("along_x", 2, 0), ("density", 1), ("along_x", 3, 0), ("out", 1),
+    ("mul", 2, 0), ("mul", 3, 0), ("near", 1), ("y", 1, 3), ("x", 2, 2), ("x", 3, 2), ("along_x", 2, 1),
+    ("along_x", 3, 1), ("far", 1), ("outs", 1), ("y", 2, 3), ("own", 4), ("start", 4), ("x", 2, 3), ("x", 3, 3),
+    ("along_x", 2, 2), ("mate", 1), ("along_x", 3, 2), ("y", 3, 0), ("new", 1), ("x", 4, 0), ("along_x", 2, 3),
+    ("along_x", 3, 3), ("y", 3, 1), ("along_z", 4, 1), ("along_z", 4, 2), ("mul", 2, 1), ("mul", 3, 1), ("mul", 2, 2),
+    ("mul", 3, 2), ("along_y", 1), ("far_x", 2), ("far_x", 3), ("x", 4, 1), ("mul", 2, 3), ("mul", 3, 3), ("sum", 2),
+    ("along_x", 4, 0), ("mul", "y", 1), ("mul", "y", 2), ("y", 3, 2), ("along_z", 4, 3), ("x", 4, 2), ("mul", 4, 0),
+    ("y", 3, 3), ("along_x", 4, 1), ("density", 2), ("out", 2), ("x", 4, 3), ("along_x", 4, 2), ("near", 2),
+    ("along_y", 2), ("far", 2), ("outs", 2), ("along_x", 4, 3), ("mul", "y", 3), ("mul", 4, 1), ("mate", 2),
+    ("mul", 4, 2), ("far_x", 4), ("new", 2), ("mul", 4, 3), ("sum", 3), ("density", 3), ("out", 3), ("outs", 3),
+)
 PIECE = 32
 CHUNK = 1024
 
@@ -89,10 +106,10 @@
     pl.semaphore_wait(barrier, len(partners))
 
     order = [0, 3, 1, 2]
-    tasks = []
-
-    def task(t, fn, cond=None):
-        tasks.append((t, fn, cond))
+    tasks = {}
+
+    def task(name, fn, cond=None):
+        tasks[name] = (fn, cond)
 
     def g(s, start, size):
         return gath.at[s, pl.ds(start, size)]
@@ -101,23 +118,27 @@
         src = g(s, block_at(zn[order[b]], x, c), BLOCK)
         send(src, src, s_a.at[s], r_x.at[s, 0, b], up_x)
         send(src, src, s_a.at[s], r_x.at[s, 1, b], down_x)
-
-    def a_start(s):
-        if s == 0:
-            load_h.wait()
-        elif s < 3:
-            @pl.when(lag >= s)
-            def _():
-                wait(g(s, own, BLOCK), r_shift.at[s])
-        if s >= 2:
-            @pl.when(lag == s - 1)
-            def _():
-                gath[s, pl.ds(own, BLOCK), :] = ob[0]
-        if s == 3:
+        if s in ROUTED:
+            send(src, src, s_a.at[s], r_x.at[s, 2, b], far_x)
+
+    def a_own(s, n=None):
+        if n is not None:
+            if s == 3:
+
+                @pl.when(lag == 2)
+                def _():
+                    gath[s, pl.ds(own, BLOCK), :] = ob[0]
+
             @pl.when(lag == 1)
             def _():
-                gath[s, pl.ds(own, BLOCK), :] = ob[1]
-
+                gath[s, pl.ds(own, BLOCK), :] = ob[n]
+
+        elif s == 0:
+            load_h.wait()
+        else:
+            wait(g(s, own, BLOCK), r_shift.at[s])
+
+    def a_start(s):
         src = g(s, own, BLOCK)
         send(src, src, s_a.at[s], r_z.at[s, 0], up_z)
         send(src, src, s_a.at[s], r_z.at[s, 1], down_z)
@@ -153,10 +174,12 @@
         zz = zn[order[b]]
         wait(g(s, block_at(zz, xn[3], c), BLOCK), r_x.at[s, 0, b])
         src = g(s, block_at(zz, xn[3], c), HALF)
-        send(src, src, s_a.at[s], r_x.at[s, 2, b], up_x)
+        if s not in ROUTED:
+            send(src, src, s_a.at[s], r_x.at[s, 2, b], up_x)
         wait(g(s, block_at(zz, xn[1], c), BLOCK), r_x.at[s, 1, b])
         src = g(s, block_at(zz, xn[1], c) + HALF, HALF)
-        send(src, src, s_a.at[s], r_x.at[s, 2, b], down_x)
+        if s not in ROUTED:
+            send(src, src, s_a.at[s], r_x.at[s, 2, b], down_x)
         if b == 3:
             to_mate(s, 1, xn[3])
             to_mate(s, 2, xn[1])
@@ -209,7 +232,7 @@
         send(zp.at[0], wv, s_w.at[0], r_w.at[0], (lag_of(1), row))
 
     def rs_send(n):
-        for k in range(1, LAGS):
+        for k in FAR_FIRST:
             to = lag_of(k)
             send(
                 part.at[n, pl.ds(pl.multiple_of(to * PIECE, PIECE), PIECE)],
@@ -235,8 +258,10 @@
             send(src, src, s_d.at[n], r_dz.at[n, 1], up_z)
             send(src, src, s_d.at[n], r_dz.at[n, 2], down_z)
             d_send_x(n, 0)
+
+    def out_send(n):
         src = ob.at[n, pl.ds(piece, PIECE)]
-        for k in range(1, LAGS):
+        for k in FAR_FIRST:
             send(src, src, s_o.at[n], r_o.at[n], (lag_of(k), row))
 
     def d_send_x(n, b):
@@ -271,70 +296,51 @@
 
     def o_ready(n):
         wait(ob.at[n, pl.ds(0, (LAGS - 1) * PIECE)], r_o.at[n])
+        store(n).start()
+
+    def store(n):
+        return pltpu.make_async_copy(ob.at[n], out_hbm.at[n], s_out.at[n])
 
     def z_ready():
         wait(zv, s_loc.at[1])
         load_e.wait()
 
-    ends = [0] * STEPS
-
-    def gather(s, tz, x_at, x_lag, cond=None):
-        def add(t, fn, *more):
-            task(t, functools.partial(fn, s, *more), cond)
-
-        add(tz, a_start)
-        for b in range(1, 4):
-            add(tz + ZT[b], a_z, b)
-        add(tz + ZT[3] + 2, multiply, 0)
+    task("shift", shift)
+    task("z", z_ready)
+    task("cut", w_cut, lag == 0)
+    task("cut_out", w_send, lag == 0)
+    task("relay", w_relay, (lag == 2) | (lag == 6))
+    low = (lag == 1) | (lag == 2)
+    gathers = ((0, None, None), (1, None, lag >= 1), (2, None, lag >= 2), (2, 0, lag == 1), (3, 1, low))
+    for i, (s, n, cond) in enumerate(gathers):
+        task(("own", i), functools.partial(a_own, s, n), cond)
+        task(("start", i), functools.partial(a_start, s), cond)
         for b in range(4):
-            add(max(x_at[b], tz + ZT[b]) + 0.001, x_send, b)
-            add(x_at[b] + x_lag, a_x, b)
-        last = x_at[3] + x_lag
-        add(last + 1.5, multiply, 1)
-        add(last + 1.6, multiply, 2)
-        add(last + 2, a_x_far)
-        add(last + 3.5, multiply, 3)
-        ends[s] = max(ends[s], last + 3.6)
-
-    gather(0, 0, X_AT[0], 5)
-    task(0.5, shift)
-    task(1, z_ready)
-    task(1.1, w_cut, lag == 0)
-    task(1.2, w_send, lag == 0)
-    task(W_RELAY, w_relay, (lag == 2) | (lag == 6))
-    gather(1, Z_AT[1], X_AT[1], X_LAG, lag >= 1)
-    gather(2, Z_AT[2], X_AT[2], X_LAG, lag >= 1)
-    gather(3, Z_AT[3], X_AT[3], X_LAG, (lag == 1) | (lag == 2))
-    blocks = [(0, b) for b in range(4)] + [(j, b) for b in range(4) for j in (1, 2)] + [(3, b) for b in range(4)]
-    for i, (j, b) in enumerate(blocks):
-        task(Y_AT[0] + Y_AT[1] * i, functools.partial(to_y, j, b), (lag >= 1) & (lag + 2 < LAGS))
+            task(("along_z", i, b), functools.partial(a_z, s, b), cond)
+            task(("x", i, b), functools.partial(x_send, s, b), cond)
+            task(("along_x", i, b), functools.partial(a_x, s, b), cond)
+        task(("far_x", i), functools.partial(a_x_far, s), cond)
+        for j in range(4):
+            task(("mul", i, j), functools.partial(multiply, s, j), cond)
+    for j in range(4):
+        task(("mul", "y", j), functools.partial(multiply, 3, j), lag >= 3)
+        for b in range(4):
+            task(("y", j, b), functools.partial(to_y, j, b), (lag >= 1) & (lag + 2 < LAGS))
     for i in range(3):
-        t = Y_AT[0] + Y_AT[1] * (3, 11, 15)[i] + Y_AT[2]
-        task(t, functools.partial(from_y, i), lag >= 3)
-        for j in ((0,), (1, 2), (3,))[i]:
-            task(t + 2, functools.partial(multiply, 3, j), lag >= 3)
-        ends[3] = max(ends[3], t + 2.1)
+        task(("along_y", i), functools.partial(from_y, i), lag >= 3)
     for n in range(STEPS):
-        ready = max(C_AT[n], ends[n])
-        task(ready, functools.partial(rs_send, n))
-        task(ready + 6, functools.partial(new_density, n))
-        task(ready + 11, functools.partial(o_ready, n))
-        if n < STEPS - 1:
-            task(ready + 9, functools.partial(d_near, n))
-            task(ready + 10.5, functools.partial(d_far, n))
-            task(ready + 14, functools.partial(d_c, n))
-            task(ready + 15.5, functools.partial(d_mul, n))
-            ends[n + 1] = max(ends[n + 1], ready + 15.6)
-            if n < 2:
-                assert Z_AT[n + 2] > ready + 11
-    for t, fn, cond in sorted(tasks, key=lambda item: item[0]):
+        for name, fn in (
+            ("sum", rs_send), ("density", new_density), ("out", out_send), ("outs", o_ready),
+            ("near", d_near), ("far", d_far), ("mate", d_c), ("new", d_mul),
+        ):
+            task((name, n), functools.partial(fn, n))
+    for name in ORDER:
+        fn, cond = tasks[name]
         if cond is None:
             fn()
         else:
             pl.when(cond)(fn)
 
-    store = pltpu.make_async_copy(ob, out_hbm, s_out.at[0])
-    store.start()
     for n in range(STEPS):
         wait(rsb.at[n, pl.ds(0, LAGS - 1)], s_rs.at[n])
         wait(ob.at[n, pl.ds(0, (LAGS - 1) * PIECE)], s_o.at[n])
@@ -370,7 +376,8 @@
     def _():
         wait(zp.at[pl.ds(0, LAGS - 1)], s_w.at[0])
 
-    store.wait()
+    for n in range(STEPS):
+        store(n).wait()
 
 
 def body(lag_matrices, history, excitation, admittance, saturation):
@@ -400,7 +407,7 @@
             dma((STEPS,)), dma((STEPS,)),
             dma((STEPS,)), dma((STEPS, 3)), dma((STEPS, 4)), dma((STEPS,)),
             dma((STEPS,)), dma((STEPS,)),
-            dma((1,)),
+            dma((STEPS,)),
         ],
         compiler_params=pltpu.CompilerParams(
             collective_id=0, has_side_effects=True, vmem_limit_bytes=60 * 1024 * 1024

time: 135 us -> 129 us (0.956)
  Pallas kernels: 133 us -> 127 us
    pallas_call x1, Pallas kernels: 133 us -> 127 us  [body(): pl.pallas_call(kernel, out_shape=jax.ShapeDtypeStruct((STEPS, BLOCK, COLS...]
where the time goes in v3:
time: 129 us
  Pallas kernels  127 us (98%)
  local copies, waits for them, and re-layouts  1.87 us (1%)
    pallas_call x1, Pallas kernels, body(): pl.pallas_call(kernel, out_shape=jax.ShapeDtypeStruct((STEPS, BLOCK, COLS...  127 us

profile of v3, /device:TPU:1, one launch (start us, length us, event | category | flops | bytes accessed | tf_op | source)
XLA Modules:
  0.0 129.3 jit_solution(14774278612848817966)
XLA Ops:
  0.0 127.4 %shard_map.55 = bf16[4,256,256]{2,1,0:T(8,128)(2,1)} custom-call(bf16[1,256,8192]{2,1,0:T(8,128)(2,1)} %z_hbm.1, bf16[1,256,256]{2,1,0:T(8,128)(2,1)} %h_hbm.1, f32[4,256,256]{2,1,0:T(8,128)} %e_hbm.1, f32[1,256]{1,0:T(1,128)} %bitcast.2, f32[1,256]{1,0:T(1,128)} %bitcast.3), custom_call_target="tpu_custom_call" | custom-call | tf_op jit(solution)/shard_map/pallas_call | solution.py:387
  127.4 1.9 %copy.7 = bf16[4,256,256]{2,1,0:T(8,128)(2,1)} copy(bf16[4,256,256]{2,1,0:T(8,128)(2,1)} %shard_map.55) | data formatting | bytes 1048576

commit v4 on v3

--- a/solution.py
+++ b/solution.py
@@ -15,26 +15,26 @@
 ROUTED = (0,)
 FAR_FIRST = (4, 5, 3, 2, 6, 1, 7)
 ORDER = (
-    ("own", 0), ("start", 0), ("x", 0, 0), "shift", "z", "cut", "cut_out", ("along_z", 0, 1), ("along_z", 0, 2),
-    ("x", 0, 1), ("own", 1), ("start", 1), ("along_z", 0, 3), ("x", 0, 2), ("mul", 0, 0), ("x", 0, 3),
-    ("along_z", 1, 1), ("along_z", 1, 2), ("x", 1, 0), ("y", 0, 0), "relay", ("along_z", 1, 3), ("y", 0, 1),
-    ("x", 1, 1), ("along_x", 0, 0), ("along_x", 0, 1), ("along_x", 0, 2), ("along_x", 0, 3), ("mul", 0, 1),
-    ("mul", 0, 2), ("far_x", 0), ("mul", 0, 3), ("sum", 0), ("y", 0, 2), ("mul", 1, 0), ("x", 1, 2), ("along_x", 1, 0),
-    ("y", 0, 3), ("x", 1, 3), ("along_x", 1, 1), ("density", 0), ("out", 0), ("y", 1, 0), ("near", 0),
-    ("along_x", 1, 2), ("y", 2, 0), ("far", 0), ("outs", 0), ("own", 2), ("start", 2), ("own", 3), ("start", 3),
-    ("y", 1, 1), ("along_x", 1, 3), ("mate", 0), ("along_y", 0), ("mul", 1, 1), ("new", 0), ("mul", 1, 2), ("far_x", 1),
-    ("mul", "y", 0), ("y", 2, 1), ("mul", 1, 3), ("sum", 1), ("x", 2, 0), ("x", 3, 0), ("along_z", 2, 1),
-    ("along_z", 3, 1), ("along_z", 2, 2), ("along_z", 3, 2), ("y", 1, 2), ("x", 2, 1), ("x", 3, 1), ("y", 2, 2),
-    ("along_z", 2, 3), ("along_z", 3, 3), ("along_x", 2, 0), ("density", 1), ("along_x", 3, 0), ("out", 1),
-    ("mul", 2, 0), ("mul", 3, 0), ("near", 1), ("y", 1, 3), ("x", 2, 2), ("x", 3, 2), ("along_x", 2, 1),
-    ("along_x", 3, 1), ("far", 1), ("outs", 1), ("y", 2, 3), ("own", 4), ("start", 4), ("x", 2, 3), ("x", 3, 3),
-    ("along_x", 2, 2), ("mate", 1), ("along_x", 3, 2), ("y", 3, 0), ("new", 1), ("x", 4, 0), ("along_x", 2, 3),
-    ("along_x", 3, 3), ("y", 3, 1), ("along_z", 4, 1), ("along_z", 4, 2), ("mul", 2, 1), ("mul", 3, 1), ("mul", 2, 2),
-    ("mul", 3, 2), ("along_y", 1), ("far_x", 2), ("far_x", 3), ("x", 4, 1), ("mul", 2, 3), ("mul", 3, 3), ("sum", 2),
-    ("along_x", 4, 0), ("mul", "y", 1), ("mul", "y", 2), ("y", 3, 2), ("along_z", 4, 3), ("x", 4, 2), ("mul", 4, 0),
-    ("y", 3, 3), ("along_x", 4, 1), ("density", 2), ("out", 2), ("x", 4, 3), ("along_x", 4, 2), ("near", 2),
-    ("along_y", 2), ("far", 2), ("outs", 2), ("along_x", 4, 3), ("mul", "y", 3), ("mul", 4, 1), ("mate", 2),
-    ("mul", 4, 2), ("far_x", 4), ("new", 2), ("mul", 4, 3), ("sum", 3), ("density", 3), ("out", 3), ("outs", 3),
+    ("own", 0), ("start", 0), ("x", 0, 0), "shift", "z", "cut", "cut_out", ("along_z", 0, 1), ("x", 0, 1),
+    ("along_z", 0, 2), ("x", 0, 2), ("own", 1), ("start", 1), ("along_z", 0, 3), ("x", 0, 3), ("mul", 0, 0),
+    ("x", 1, 0), ("along_z", 1, 1), ("along_z", 1, 2), ("x", 1, 1), ("y", 0, 0), "relay", ("along_z", 1, 3),
+    ("y", 0, 1), ("x", 1, 2), ("along_x", 0, 0), ("along_x", 0, 1), ("along_x", 0, 2), ("along_x", 0, 3), ("mul", 0, 1),
+    ("mul", 0, 2), ("far_x", 0), ("mul", 0, 3), ("sum", 0), ("y", 0, 2), ("mul", 1, 0), ("x", 1, 3), ("along_x", 1, 0),
+    ("y", 0, 3), ("along_x", 1, 1), ("density", 0), ("out", 0), ("y", 1, 0), ("near", 0), ("along_x", 1, 2),
+    ("y", 2, 0), ("far", 0), ("outs", 0), ("own", 2), ("start", 2), ("own", 3), ("start", 3), ("y", 1, 1),
+    ("along_x", 1, 3), ("mate", 0), ("along_y", 0), ("mul", 1, 1), ("new", 0), ("mul", 1, 2), ("far_x", 1), ("x", 2, 0),
+    ("x", 3, 0), ("mul", "y", 0), ("y", 2, 1), ("mul", 1, 3), ("sum", 1), ("along_z", 2, 1), ("x", 2, 1),
+    ("along_z", 3, 1), ("x", 3, 1), ("along_z", 2, 2), ("along_z", 3, 2), ("y", 1, 2), ("x", 2, 2), ("x", 3, 2),
+    ("y", 2, 2), ("along_z", 2, 3), ("along_z", 3, 3), ("along_x", 2, 0), ("density", 1), ("along_x", 3, 0), ("out", 1),
+    ("mul", 2, 0), ("mul", 3, 0), ("near", 1), ("y", 1, 3), ("x", 2, 3), ("x", 3, 3), ("along_x", 2, 1),
+    ("along_x", 3, 1), ("far", 1), ("outs", 1), ("y", 2, 3), ("own", 4), ("start", 4), ("along_x", 2, 2), ("mate", 1),
+    ("along_x", 3, 2), ("y", 3, 0), ("new", 1), ("x", 4, 0), ("along_x", 2, 3), ("along_x", 3, 3), ("y", 3, 1),
+    ("along_z", 4, 1), ("along_z", 4, 2), ("mul", 2, 1), ("mul", 3, 1), ("mul", 2, 2), ("mul", 3, 2), ("along_y", 1),
+    ("far_x", 2), ("far_x", 3), ("x", 4, 1), ("mul", 2, 3), ("mul", 3, 3), ("sum", 2), ("along_x", 4, 0),
+    ("mul", "y", 1), ("mul", "y", 2), ("y", 3, 2), ("along_z", 4, 3), ("x", 4, 2), ("mul", 4, 0), ("y", 3, 3),
+    ("along_x", 4, 1), ("density", 2), ("out", 2), ("x", 4, 3), ("along_x", 4, 2), ("near", 2), ("along_y", 2),
+    ("far", 2), ("outs", 2), ("along_x", 4, 3), ("mul", "y", 3), ("mul", 4, 1), ("mate", 2), ("mul", 4, 2),
+    ("far_x", 4), ("new", 2), ("mul", 4, 3), ("sum", 3), ("density", 3), ("out", 3), ("outs", 3),
 )
 PIECE = 32
 CHUNK = 1024

time: 129 us -> 129 us (level)
  no operation moved by 1% of the time
where the time goes in v4:
time: 129 us
  Pallas kernels  127 us (98%)
  local copies, waits for them, and re-layouts  1.87 us (1%)
    pallas_call x1, Pallas kernels, body(): pl.pallas_call(kernel, out_shape=jax.ShapeDtypeStruct((STEPS, BLOCK, COLS...  127 us

profile of v4, /device:TPU:1, one launch (start us, length us, event | category | flops | bytes accessed | tf_op | source)
XLA Modules:
  0.0 128.5 jit_solution(16791899338709538035)
XLA Ops:
  0.0 126.7 %shard_map.55 = bf16[4,256,256]{2,1,0:T(8,128)(2,1)} custom-call(bf16[1,256,8192]{2,1,0:T(8,128)(2,1)} %z_hbm.1, bf16[1,256,256]{2,1,0:T(8,128)(2,1)} %h_hbm.1, f32[4,256,256]{2,1,0:T(8,128)} %e_hbm.1, f32[1,256]{1,0:T(1,128)} %bitcast.2, f32[1,256]{1,0:T(1,128)} %bitcast.3), custom_call_target="tpu_custom_call" | custom-call | tf_op jit(solution)/shard_map/pallas_call | solution.py:387
  126.7 1.9 %copy.7 = bf16[4,256,256]{2,1,0:T(8,128)(2,1)} copy(bf16[4,256,256]{2,1,0:T(8,128)(2,1)} %shard_map.55) | data formatting | bytes 1048576
